TPU v7x, 32 devices: a whole 2x2x4 slice. The times are simulated.
32 devices in a mesh: chan: 16 (over z, y, x), day: 2 (over core).
Axes of the slice: x: 2, y: 2, z: 4, core: 2. Of those that a mesh axis runs over, the one named last changes fastest.
Arguments:
- spectra: bfloat16 [512, 64, 400], P('chan', 'day'), may hold values from -6 to 6
- owners: int32 [2], replicated, may hold values from 0 to 15
Outputs:
- stacks: bfloat16 [2, 512, 32, 400], P(None, ('chan', 'day'))
Inputs may be any that keep to these rules, and one draw needn't show every extreme that they name: `owners`: block indices along the channel axis; two steps may name the same block.
All inputs are finite; a program needn't handle non-finite values.
Results may differ from a plain program's by a relative error of at most 0.0073.
Values may be sent and summed in bfloat16 or wider, within the bound.
A program may use at most 64 MiB of HBM per device.

v0:
```python
import math
import jax
import jax.numpy as jnp
from jax import lax
from jax.sharding import PartitionSpec as P

LAGS = 400
STEPS = 2


def broadcast(array, axis, root):
    mine = lax.axis_index(axis) == root
    return lax.psum(jnp.where(mine, array, jnp.zeros_like(array)), axis)


def whiten(spectra, bins):
    values = spectra.astype(jnp.float32)
    real_part = values[..., :bins]
    imag_part = values[..., bins:]
    power = real_part * real_part + imag_part * imag_part
    mean_power = jnp.mean(power, axis=-1, keepdims=True)
    factor = lax.rsqrt(power + 0.25 * mean_power + 1e-06)
    return jnp.concatenate([real_part * factor, imag_part * factor], axis=-1).astype(jnp.bfloat16)


def lag_table(bins, lag_count):
    freqs = jnp.arange(bins, dtype=jnp.int32)
    shifts = jnp.arange(lag_count, dtype=jnp.int32) - lag_count // 2
    phase = jnp.mod(freqs[:, None] * shifts[None, :], 2 * bins)
    angle = phase.astype(jnp.float32) * (math.pi / bins)
    return jnp.concatenate([jnp.cos(angle), -jnp.sin(angle)], axis=0).astype(jnp.bfloat16)


def day_cross(own, other, bins):
    own_re, own_im = (own[..., :bins], own[..., bins:])
    oth_re, oth_im = (other[..., :bins], other[..., bins:])
    cross_re = jnp.einsum("iwf,jwf->ijf", own_re, oth_re, preferred_element_type=jnp.float32)
    cross_re = cross_re + jnp.einsum(
        "iwf,jwf->ijf", own_im, oth_im, preferred_element_type=jnp.float32
    )
    cross_im = jnp.einsum("iwf,jwf->ijf", own_im, oth_re, preferred_element_type=jnp.float32)
    cross_im = cross_im - jnp.einsum(
        "iwf,jwf->ijf", own_re, oth_im, preferred_element_type=jnp.float32
    )
    cross = jnp.concatenate([cross_re, cross_im], axis=-1).astype(jnp.bfloat16)
    return cross.astype(jnp.float32)


def apply_lags(summed, table, norm):
    kept = summed.astype(jnp.bfloat16)
    rows = kept.shape[0] * kept.shape[1]
    lagged = (
        jnp.dot(kept.reshape(rows, kept.shape[2]), table, preferred_element_type=jnp.float32) * norm
    )
    return lagged.reshape(kept.shape[0], kept.shape[1], table.shape[1]).astype(jnp.bfloat16)


def local(spectra, owners):
    bins = spectra.shape[-1] // 2
    windows_all = spectra.shape[1] * lax.axis_size("day")
    white = whiten(spectra, bins)
    table = lag_table(bins, LAGS)
    norm = 1.0 / math.sqrt(windows_all * bins)
    result_steps = []
    for step in range(STEPS):
        block = broadcast(white, "chan", owners[step])
        crossed = day_cross(white, block, bins)
        summed = lax.psum_scatter(
            crossed.astype(jnp.bfloat16), "day", scatter_dimension=0, tiled=True
        ).astype(jnp.float32)
        result_steps.append(apply_lags(summed, table, norm))
    return jnp.stack(result_steps, axis=0)


def solution(mesh):
    placed = (P("chan", "day", None), P())
    return jax.shard_map(
        local,
        mesh=mesh,
        in_specs=placed,
        out_specs=P(None, ("chan", "day"), None, None),
        check_vma=False,
    )
```

profile of v0, /device:TPU:0, one launch (start us, length us, event | category | flops | bytes accessed | tf_op | source)
XLA Modules:
  0.0 300.6 jit_solution(8346272925173790976)
XLA Ops:
  6.5 0.0 all-reduce.3.cloned.1.call-start
  6.5 1.5 convert_element_type.46
  8.0 0.5 fusion.13
  8.6 0.6 multiply_convert_fusion.1
  9.2 0.0 copy-start.11
  9.2 0.0 copy-start.12
  9.2 0.0 copy-start.14
  9.2 0.8 copy-done.11
  10.0 0.2 copy-done.12
  10.2 1.4 pad_maximum_fusion
  11.6 3.7 %copy.11 = bf16[32,32,400]{1,0,2:T(8,128)(2,1)S(1)} copy(bf16[32,32,400]{2,1,0:T(8,128)(2,1)} %pad_maximum_fusion) | data formatting | bytes 1638400 | tf_op jit(solution)/shard_map/concatenate | solution.py:23
  15.2 0.0 copy-done.14
  15.3 0.7 fusion.14
  17.3 3.2 %broadcast_select_fusion.1 = (bf16[32,32,400]{1,0,2:T(8,128)(2,1)}, bf16[32,32,400]{1,0,2:T(8,128)(2,1)}) fusion(bf16[32,32,400]{1,0,2:T(8,128)(2,1)S(1)} %copy.11, pred[]{:T(512)S(6)} %eq.8, pred[]{:T(512)S(6)} %eq.9), kind=kLoop, calls=%fused_computation.5 | loop fusion | flops 819200 | bytes 2457602 | tf_op jit(solution)/shard_map/jit(_where)/select_n | solution.py:13
  20.4 0.0 copy-start.13
  20.4 0.0 all-reduce.3.cloned.1.call-update
  20.4 0.0 reduce-scatter.3.cloned.1.call-start
  20.5 1.0 copy-done.13
  21.5 1.5 copy.12
  22.9 0.0 copy-start.4
  23.0 2.6 copy.13
  25.5 0.0 copy-start.6
  25.5 213.4 %all-reduce.3.cloned.1.call-done = (bf16[32,32,400]{1,0,2:T(8,128)(2,1)}, bf16[32,32,400]{1,0,2:T(8,128)(2,1)}) async-done(((bf16[32,32,400]{1,0,2:T(8,128)(2,1)}, bf16[32,32,400]{1,0,2:T(8,128)(2,1)}), (bf16[32,32,400]{1,0,2:T(8,128)(2,1)}, bf16[32,32,400]{1,0,2:T(8,128)(2,1)})) %all-reduce.3.cloned.1.call-update) | async-done | bytes 1638416 | tf_op jit(solution)/shard_map/psum | solution.py:13
  238.9 0.0 copy-start.2
  238.9 4.2 %fusion.15 = f32[200,32,32]{2,1,0:T(8,128)} fusion(bf16[32,32,400]{1,0,2:T(8,128)(2,1)} %get-tuple-element.6, bf16[32,32,200]{1,0,2:T(8,128)(2,1)S(1)} %copy.12), kind=kOutput, calls=%fused_computation.38 | convolution fusion | flops 13107200 | bytes 2048000 | tf_op jit(solution)/shard_map/iwf,jwf->ijf/dot_general | solution.py:37
  243.2 0.0 copy-done.6
  243.2 0.0 copy-done.2
  243.2 0.0 copy-start
  243.2 2.7 fusion.16
  245.8 0.0 copy-done.4
  245.8 0.0 copy-done
  245.8 0.0 copy-start.7
  245.8 2.7 fusion.17
  248.5 0.0 copy-done.7
  248.6 2.7 fusion.18
  251.3 0.0 copy-done.3
  251.3 1.4 copy-done.9
  252.7 2.1 fusion
  254.8 3.8 %copy.16 = bf16[32,32,200]{2,1,0:T(8,128)(2,1)} copy(bf16[32,32,200]{0,1,2:T(8,128)(2,1)} %fusion) | data formatting | bytes 819200 | tf_op jit(solution)/shard_map/add | solution.py:38
  258.6 4.6 %fusion.1 = bf16[32,32,200]{0,1,2:T(8,128)(2,1)} fusion(f32[200,32,32]{2,1,0:T(8,128)} %fusion.16, bf16[32,32,400]{1,0,2:T(8,128)(2,1)S(1)} %copy-done.3, bf16[32,32,200]{1,0,2:T(8,128)(2,1)} %copy-done.4), kind=kOutput, calls=%fused_computation.7 | convolution fusion | flops 13516800 | bytes 2457600 | tf_op jit(solution)/shard_map/iwf,jwf->ijf/dot_general | solution.py:42
  263.2 4.0 %copy.17 = bf16[32,32,200]{2,1,0:T(8,128)(2,1)} copy(bf16[32,32,200]{0,1,2:T(8,128)(2,1)} %fusion.1) | data formatting | bytes 819200 | tf_op jit(solution)/shard_map/sub | solution.py:42
  267.2 2.6 pad_maximum_fusion.1
  269.8 0.0 reduce-scatter.3.cloned.1.call-update
  269.8 0.2 reduce-scatter.5.cloned.1.call-start
  270.0 0.0 copy-done.1
  270.0 0.0 copy-start.5
  270.1 0.0 copy-start.8
  270.1 4.7 %fusion.2 = bf16[32,32,200]{0,1,2:T(8,128)(2,1)} fusion(f32[200,32,32]{2,1,0:T(8,128)} %fusion.17, bf16[32,32,400]{1,0,2:T(8,128)(2,1)S(1)} %copy-done.1, bf16[32,32,200]{1,0,2:T(8,128)(2,1)} %copy-done.6), kind=kOutput, calls=%fused_computation.8 | convolution fusion | flops 13516800 | bytes 2457600 | tf_op jit(solution)/shard_map/iwf,jwf->ijf/dot_general | solution.py:38
  274.8 0.0 copy-done.5
  274.8 0.0 copy-done.8
  274.8 2.1 fusion.3
  276.9 3.3 %copy.24 = bf16[32,32,200]{2,1,0:T(8,128)(2,1)S(1)} copy(bf16[32,32,200]{0,1,2:T(8,128)(2,1)} %fusion.2) | data formatting | bytes 819200 | tf_op jit(solution)/shard_map/add | solution.py:38
  280.2 0.0 copy-done.10
  280.3 1.9 copy.25
  282.1 1.4 pad_maximum_fusion.2
  283.5 0.0 reduce-scatter.5.cloned.1.call-update
  283.6 1.8 cosine_convert_fusion
  285.3 0.0 reduce-scatter.3.cloned.1.call-done
  285.4 1.5 fusion.4
  286.8 0.2 copy.18
  287.1 4.2 %reduce-scatter.5.cloned.1.call-done = bf16[16,32,400]{2,1,0:T(8,128)(2,1)} async-done(((bf16[32,32,400]{2,1,0:T(8,128)(2,1)}), bf16[16,32,400]{2,1,0:T(8,128)(2,1)}) %reduce-scatter.5.cloned.1.call-update) | async-done | bytes 409616 | tf_op jit(solution)/shard_map/reduce_scatter | solution.py:68
  291.2 1.5 fusion.5
  292.7 0.2 copy.26
  292.9 1.1 pad_maximum_fusion.3
  (6 shorter events, 0.0 us)
Async XLA Ops:
  6.5 232.4 %all-reduce.3.cloned.1.call-start = ((), (), s32[]{:S(2)}) async-start(), calls=%async_computation.4 | async-start | bytes 13107200 | tf_op jit(solution)/shard_map/psum | solution.py:13
  9.2 0.8 copy-start.11
  9.2 1.0 copy-start.12
  9.2 6.0 %copy-start.14 = (s32[2]{0:T(128)S(1)}, s32[2]{0:T(128)}, u32[]{:S(2)}) copy-start(s32[2]{0:T(128)} %param.3) | copy-start | bytes 28
  20.4 1.0 copy-start.13
  20.4 264.9 %reduce-scatter.3.cloned.1.call-start = ((), (), s32[]{:S(2)}) async-start(), calls=%async_computation.2 | async-start | bytes 1572864 | tf_op jit(solution)/shard_map/reduce_scatter | solution.py:68
  22.9 222.9 %copy-start.4 = (bf16[32,32,200]{1,0,2:T(8,128)(2,1)}, bf16[32,32,200]{1,0,2:T(8,128)(2,1)S(1)}, u32[]{:S(2)}) copy-start(bf16[32,32,200]{1,0,2:T(8,128)(2,1)S(1)} %copy.12) | copy-start | bytes 1228804
  25.5 217.6 %copy-start.6 = (bf16[32,32,200]{1,0,2:T(8,128)(2,1)}, bf16[32,32,200]{1,0,2:T(8,128)(2,1)S(1)}, u32[]{:S(2)}) copy-start(bf16[32,32,200]{1,0,2:T(8,128)(2,1)S(1)} %copy.13) | copy-start | bytes 1228804
  238.9 4.2 %copy-start.2 = (bf16[32,32,400]{1,0,2:T(8,128)(2,1)S(1)}, bf16[32,32,400]{1,0,2:T(8,128)(2,1)}, u32[]{:S(2)}) copy-start(bf16[32,32,400]{1,0,2:T(8,128)(2,1)} %get-tuple-element.6) | copy-start | bytes 2457604
  243.2 2.7 copy-start
  245.8 2.7 copy-start.7
  248.5 2.7 copy-start.3
  248.5 4.1 %copy-start.9 = (f32[200,32,32]{2,1,0:T(8,128)S(1)}, f32[200,32,32]{2,1,0:T(8,128)}, u32[]{:S(2)}) copy-start(f32[200,32,32]{2,1,0:T(8,128)} %fusion.15) | copy-start | bytes 2457604
  263.2 6.9 %copy-start.1 = (bf16[32,32,400]{1,0,2:T(8,128)(2,1)S(1)}, bf16[32,32,400]{1,0,2:T(8,128)(2,1)}, u32[]{:S(2)}) copy-start(bf16[32,32,400]{1,0,2:T(8,128)(2,1)} %get-tuple-element.5) | copy-start | bytes 2457604
  269.8 21.4 %reduce-scatter.5.cloned.1.call-start = ((), (), s32[]{:S(2)}) async-start(), calls=%async_computation.3 | async-start | bytes 1572864 | tf_op jit(solution)/shard_map/reduce_scatter | solution.py:68
  270.0 4.7 %copy-start.5 = (bf16[32,32,200]{1,0,2:T(8,128)(2,1)S(1)}, bf16[32,32,200]{1,0,2:T(8,128)(2,1)}, u32[]{:S(2)}) copy-start(bf16[32,32,200]{1,0,2:T(8,128)(2,1)} %copy-done.4) | copy-start | bytes 1228804
  270.1 4.7 %copy-start.8 = (f32[200,32,32]{2,1,0:T(8,128)S(1)}, f32[200,32,32]{2,1,0:T(8,128)}, u32[]{:S(2)}) copy-start(f32[200,32,32]{2,1,0:T(8,128)} %fusion.18) | copy-start | bytes 2457604
  276.9 3.3 %copy-start.10 = (bf16[32,32,200]{0,1,2:T(8,128)(2,1)S(1)}, bf16[32,32,200]{0,1,2:T(8,128)(2,1)}, u32[]{:S(2)}) copy-start(bf16[32,32,200]{0,1,2:T(8,128)(2,1)} %fusion.3) | copy-start | bytes 1228804
Sparse Core Ops, SparseCore 0:
  20.6 218.3 all-reduce.2
  269.9 7.4 reduce-scatter.2
  283.7 7.5 reduce-scatter.4
where the time goes:
time: 301 us
  waiting for transfers between devices  218 us (72%)
  matrix products  28.8 us (10%)
  local copies, waits for them, and re-layouts  25.2 us (8%)
  between operations  14.7 us (5%)
  other arithmetic  14 us (5%)
    psum x1, waiting for transfers between devices, broadcast(): return lax.psum(jnp.where(mine, array, jnp.zeros_like(array)), axis)  213 us
    add x2, local copies, waits for them, and re-layouts, day_cross(): cross_re + jnp.einsum('iwf,jwf->ijf', own_im, oth_im, preferred_element_t...  7.15 us
    dot_general x2, matrix products, day_cross(): jnp.einsum('iwf,jwf->ijf', own_re, oth_re, preferred_element_type=jnp.flo...  6.94 us
    dot_general x2, matrix products, day_cross(): jnp.einsum('iwf,jwf->ijf', own_im, oth_im, preferred_element_type=jnp.flo...  6.86 us
    dot_general x2, matrix products, day_cross(): jnp.einsum('iwf,jwf->ijf', own_re, oth_im, preferred_element_type=jnp.flo...  6.69 us
  transfers between devices with their start and end apart: 3, of which 2 were waited for; matrix products, arithmetic and copies ran while one was open for 7% of the time, Pallas kernels for 0%

commit v1 on v0

--- a/solution.py
+++ b/solution.py
@@ -10,7 +10,7 @@
 
 def broadcast(array, axis, root):
     mine = lax.axis_index(axis) == root
-    return lax.psum(jnp.where(mine, array, jnp.zeros_like(array)), axis)
+    return jnp.sum(lax.all_gather(jnp.where(mine, array, jnp.zeros_like(array)), axis), axis=0)
 
 
 def whiten(spectra, bins):

time: 301 us -> 450 us (1.50)
  waiting for transfers between devices: 218 us -> 346 us
  other arithmetic: 14 us -> 32.2 us
  local copies, waits for them, and re-layouts: 25.2 us -> 36.2 us
  matrix products: 28.8 us -> 20.5 us
    all_gather x0 -> x2, waiting for transfers between devices: none -> 342 us  [broadcast(): lax.all_gather(jnp.where(mine, array, jnp.zeros_like(array)), axis)]
    psum x1 -> x0, waiting for transfers between devices: 213 us -> none  [broadcast(): return lax.psum(jnp.where(mine, array, jnp.zeros_like(array)), axis)]
    reduce_sum x0 -> x2, other arithmetic: none -> 20.8 us  [broadcast(): jnp.sum(lax.all_gather(jnp.where(mine, array, jnp.zeros_like(array)), axi...]
    unnamed x30 -> x18, local copies, waits for them, and re-layouts: 3.37 us -> 12.7 us
  transfers between devices with their start and end apart: 3 -> 4, of which waited for: 2 -> 3; matrix products, arithmetic and copies ran while one was open for 7% -> 18% of each run, Pallas kernels for 0% -> 0%
where the time goes in v1:
time: 450 us
  waiting for transfers between devices  346 us (77%)
  local copies, waits for them, and re-layouts  36.2 us (8%)
  other arithmetic  32.2 us (7%)
  matrix products  20.5 us (5%)
  between operations  14.6 us (3%)
    all_gather x2, waiting for transfers between devices, broadcast(): lax.all_gather(jnp.where(mine, array, jnp.zeros_like(array)), axis)  342 us
    reduce_sum x2, other arithmetic, broadcast(): jnp.sum(lax.all_gather(jnp.where(mine, array, jnp.zeros_like(array)), axi...  20.8 us
    unnamed x18, local copies, waits for them, and re-layouts  12.7 us
  transfers between devices with their start and end apart: 4, of which 3 were waited for; matrix products, arithmetic and copies ran while one was open for 18% of the time, Pallas kernels for 0%

profile of v1, /device:TPU:0, one launch (start us, length us, event | category | flops | bytes accessed | tf_op | source)
XLA Modules:
  0.0 449.7 jit_solution(9655526149638644921)
XLA Ops:
  6.5 0.0 all-gather.3.cloned.1.call-start
  6.5 1.5 convert_element_type.61
  8.0 0.5 fusion.13
  8.6 0.0 copy-start.6
  8.6 0.6 multiply_convert_fusion.1
  9.2 0.0 copy-start.4
  9.2 0.0 copy-done.6
  9.2 0.7 fusion.16
  11.2 1.9 broadcast_select_fusion.1
  13.1 0.0 all-gather.3.cloned.1.call-update
  13.2 0.0 copy-done.4
  13.2 0.0 all-gather.5.cloned.1.call-start
  13.2 0.7 all-gather.5.cloned.1.call-update
  13.9 0.0 reduce-scatter.3.cloned.1.call-start
  14.0 1.5 copy.26
  15.5 2.4 copy.28
  17.9 189.2 %all-gather.3.cloned.1.call-done = bf16[16,32,32,400]{3,2,1,0:T(8,128)(2,1)} async-done(((bf16[1,32,32,400]{3,2,1,0:T(8,128)(2,1)}), bf16[16,32,32,400]{3,2,1,0:T(8,128)(2,1)}) %all-gather.3.cloned.1.call-update) | async-done | bytes 13107216 | tf_op jit(solution)/shard_map/all_gather | solution.py:13
  207.0 10.3 %reduce_sum.34 = bf16[32,32,400]{2,1,0:T(8,128)(2,1)} reduce(bf16[16,32,32,400]{3,2,1,0:T(8,128)(2,1)} %all-gather.3.cloned.1.call-done, bf16[]{:T(256)} %constant.32.clone.1), dimensions={0}, to_apply=%region_1.2 | reduce | flops 6144000 | bytes 13926402 | tf_op jit(solution)/shard_map/reduce_sum | solution.py:13
  217.4 2.5 fusion.14
  219.9 3.2 copy.43
  223.1 3.2 copy.44
  226.2 0.0 copy-start.2
  226.2 2.5 fusion.17
  228.8 0.0 copy-done.2
  228.8 2.2 fusion
  230.9 3.9 copy.31
  234.8 0.0 copy-start.3
  234.8 2.5 fusion.18
  237.4 0.0 copy-done.3
  237.4 2.2 fusion.1
  239.5 3.8 copy.32
  243.4 2.6 pad_maximum_fusion.1
  246.0 0.0 reduce-scatter.3.cloned.1.call-update
  246.0 0.2 reduce-scatter.5.cloned.1.call-start
  246.2 152.8 %all-gather.5.cloned.1.call-done = bf16[16,32,32,400]{3,2,1,0:T(8,128)(2,1)} async-done(((bf16[1,32,32,400]{3,2,1,0:T(8,128)(2,1)}), bf16[16,32,32,400]{3,2,1,0:T(8,128)(2,1)}) %all-gather.5.cloned.1.call-update) | async-done | bytes 13107216 | tf_op jit(solution)/shard_map/all_gather | solution.py:13
  399.0 10.5 %reduce_sum.35 = bf16[32,32,400]{2,1,0:T(8,128)(2,1)} reduce(bf16[16,32,32,400]{3,2,1,0:T(8,128)(2,1)} %all-gather.5.cloned.1.call-done, bf16[]{:T(256)} %constant.32.clone.1), dimensions={0}, to_apply=%region_3.4 | reduce | flops 6144000 | bytes 13926402 | tf_op jit(solution)/shard_map/reduce_sum | solution.py:13
  409.5 2.5 fusion.15
  412.0 3.2 copy.45
  415.1 3.2 copy.46
  418.3 0.0 copy-start
  418.3 2.5 fusion.19
  420.8 0.0 copy-done
  420.8 2.2 fusion.2
  423.0 3.8 copy.40
  426.8 0.0 copy-start.1
  426.9 2.5 fusion.20
  429.4 0.0 copy-done.1
  429.4 1.0 fusion.3
  430.4 0.0 copy-start.5
  430.4 1.9 copy.41
  432.2 0.0 copy-done.5
  432.3 1.4 pad_maximum_fusion.2
  433.7 0.0 reduce-scatter.5.cloned.1.call-update
  433.7 1.8 cosine_convert_fusion
  435.5 0.0 reduce-scatter.3.cloned.1.call-done
  435.5 1.5 fusion.4
  437.0 0.2 copy.33
  437.2 3.2 reduce-scatter.5.cloned.1.call-done
  440.4 1.5 fusion.5
  441.9 0.2 copy.42
  442.1 1.1 pad_maximum_fusion.3
  (2 shorter events, 0.0 us)
Async XLA Ops:
  6.5 200.5 %all-gather.3.cloned.1.call-start = ((), (), s32[]{:S(2)}) async-start(), calls=%async_computation.2 | async-start | bytes 17825792 | tf_op jit(solution)/shard_map/all_gather | solution.py:13
  8.6 0.7 copy-start.6
  9.2 4.0 copy-start.4
  13.2 385.8 %all-gather.5.cloned.1.call-start = ((), (), s32[]{:S(2)}) async-start(), calls=%async_computation.4 | async-start | bytes 17825792 | tf_op jit(solution)/shard_map/all_gather | solution.py:13
  13.9 421.5 %reduce-scatter.3.cloned.1.call-start = ((), (), s32[]{:S(2)}) async-start(), calls=%async_computation.3 | async-start | bytes 1572864 | tf_op jit(solution)/shard_map/reduce_scatter | solution.py:68
  226.2 2.5 copy-start.2
  234.8 2.5 copy-start.3
  246.0 194.4 %reduce-scatter.5.cloned.1.call-start = ((), (), s32[]{:S(2)}) async-start(), calls=%async_computation.5 | async-start | bytes 1572864 | tf_op jit(solution)/shard_map/reduce_scatter | solution.py:68
  418.3 2.5 copy-start
  426.8 2.5 copy-start.1
  430.4 1.9 copy-start.5
Sparse Core Ops, SparseCore 0:
  13.3 193.7 all-gather.2
  209.8 189.1 all-gather.4
  401.3 6.5 reduce-scatter.2
  433.8 6.5 reduce-scatter.4
